TPU v7x, 32 devices: a whole 2x2x4 slice. The times are simulated.
32 devices in a mesh: groups: 2 (over y), context: 16 (over z, x, core).
Axes of the slice: x: 2, y: 2, z: 4, core: 2. Of those that a mesh axis runs over, the one named last changes fastest.
Arguments:
- queries: bfloat16 [8192, 8192], P(('groups', 'context')), parts along dimension 0, may hold values from -68 to 68
- keys: bfloat16 [8192, 1024], P(('groups', 'context')), parts along dimension 0, may hold values from -6 to 6
- values: bfloat16 [8192, 1024], P(('groups', 'context')), parts along dimension 0, may hold values from -6 to 6
- segments: int32 [8192], P(('groups', 'context')), parts along dimension 0, may hold values from 0 to 9, never falling along the last dimension, each value on 1 to 768 neighbouring positions
Outputs:
- rotated: bfloat16 [8192, 8192], P(('groups', 'context')), parts along dimension 0
There are 2 independent parts, one for each index of `groups`. A program takes and returns all parts, laid end to end along the dimension named above; each array names one. Nothing has to cross between parts.
Inputs may be any that keep to these rules, and one draw needn't show every extreme that they name: `segments`: document numbers never fall along the block; each document holds 1 to 768 tokens and one holds exactly 768.
All inputs are finite; a program needn't handle non-finite values.
Results may differ from a plain program's by a relative error of at most 0.0054.
Values may be sent and summed in bfloat16 or wider, within the bound.
A program may use at most 64 MiB of HBM per device.

v0:
```python
import jax
import jax.numpy as jnp
from jax import lax
from jax.sharding import PartitionSpec as P

HEADS = 64
KVH = 8
HD = 128
PRIOR = 3


def passed_along(array, axis, by):
    size = lax.axis_size(axis)
    pairs = [(i, i + by) for i in range(size) if 0 <= i + by < size]
    return lax.ppermute(array, axis, pairs)


def build_mixer(heads):
    rows = jnp.arange(heads, dtype=jnp.int32)[:, None]
    cols = jnp.arange(heads, dtype=jnp.int32)[None, :]
    both = jnp.bitwise_and(rows, cols)
    parity = jnp.zeros((heads, heads), jnp.int32)
    for level in range(heads.bit_length()):
        parity = parity + jnp.bitwise_and(jnp.right_shift(both, level), 1)
    signs = 1.0 - 2.0 * jnp.bitwise_and(parity, 1).astype(jnp.float32)
    return (signs / jnp.sqrt(jnp.float32(heads))).astype(jnp.bfloat16)


def attend(query_rows, seg_rows, key_rows, value_rows, seg_keys, offset):
    count = query_rows.shape[0]
    length = key_rows.shape[0]
    group = HEADS // KVH
    query_idx = jnp.arange(count, dtype=jnp.int32)[:, None] + offset
    key_idx = jnp.arange(length, dtype=jnp.int32)[None, :]
    allowed = (seg_keys[None, :] == seg_rows[:, None]) & (key_idx <= query_idx)
    query_heads = jnp.transpose(query_rows.reshape(count, KVH, group, HD), (1, 0, 2, 3))
    key_heads = jnp.transpose(key_rows.reshape(length, KVH, HD), (1, 0, 2))
    value_heads = jnp.transpose(value_rows.reshape(length, KVH, HD), (1, 0, 2))

    def one_head(items):
        qh, kh, vh = items
        scores = jnp.einsum("tqd,ld->qtl", qh, kh, preferred_element_type=jnp.float32) / jnp.sqrt(
            jnp.float32(HD)
        )
        masked = jnp.where(allowed[None], scores, -jnp.inf)
        top = jnp.max(masked, axis=-1, keepdims=True)
        weights = jnp.where(allowed[None], jnp.exp(scores - top), 0.0)
        total = jnp.sum(weights, axis=-1, keepdims=True)
        probs = weights.astype(jnp.bfloat16)
        summed = jnp.einsum("qtl,ld->tqd", probs, vh, preferred_element_type=jnp.float32)
        return summed / jnp.transpose(total, (1, 0, 2))

    outs = lax.map(one_head, (query_heads, key_heads, value_heads))
    attended = jnp.transpose(outs, (1, 0, 2, 3)).reshape(count, HEADS, HD).astype(jnp.bfloat16)
    mixed = jnp.einsum(
        "hk,tkd->thd", build_mixer(HEADS), attended, preferred_element_type=jnp.float32
    )
    return mixed.astype(jnp.bfloat16).reshape(count, HEADS * HD)


def per_device(queries, keys, values, segments):
    tok_rows = queries.shape[0]
    seg_plus = segments + 1
    local = (keys, values, seg_plus)
    pieces = []
    for distance in range(PRIOR, 0, -1):
        pieces.append(passed_along((local[0], local[1], local[2]), "context", distance))
    pieces.append(local)
    window = tuple((jnp.concatenate([piece[slot] for piece in pieces], 0) for slot in range(3)))
    key_win, value_win, seg_win = window
    return attend(queries, seg_plus, key_win, value_win, seg_win, PRIOR * tok_rows)


def solution(mesh):
    return jax.shard_map(
        per_device,
        mesh=mesh,
        in_specs=(
            P(("groups", "context"), None),
            P(("groups", "context"), None),
            P(("groups", "context"), None),
            P(("groups", "context")),
        ),
        out_specs=P(("groups", "context"), None),
        check_vma=False,
    )
```

profile of v0, /device:TPU:24, one launch (start us, length us, event | category | flops | bytes accessed | tf_op | source)
XLA Modules:
  0.0 178.6 jit_solution(13749500059064146118)
XLA Ops:
  0.0 2.8 %collective-permute-start = (bf16[256,1024]{1,0:T(8,128)(2,1)}, bf16[256,1024]{1,0:T(8,128)(2,1)S(1)}, u32[]{:S(2)}, u32[]{:S(2)}) collective-permute-start(bf16[256,1024]{1,0:T(8,128)(2,1)} %param.8), channel_id=1, source_target_pairs={{0,3},{1,4},{2,5},{3,6},{4,7},{5,8},{6,9},{7,10},{8,11},{9,12},{10... | collective-permute-start | bytes 1572872 | tf_op jit(solution)/shard_map/ppermute | solution.py:15
  2.8 1.9 %collective-permute-start.1 = (bf16[256,1024]{1,0:T(8,128)(2,1)}, bf16[256,1024]{1,0:T(8,128)(2,1)S(1)}, u32[]{:S(2)}, u32[]{:S(2)}) collective-permute-start(bf16[256,1024]{1,0:T(8,128)(2,1)} %param.8), channel_id=1, source_target_pairs={{0,2},{1,3},{2,4},{3,5},{4,6},{5,7},{6,8},{7,9},{8,10},{9,11},{10,... | collective-permute-start | bytes 1572872 | tf_op jit(solution)/shard_map/ppermute | solution.py:15
  4.8 1.9 %collective-permute-start.2 = (bf16[256,1024]{1,0:T(8,128)(2,1)}, bf16[256,1024]{1,0:T(8,128)(2,1)}, u32[]{:S(2)}, u32[]{:S(2)}) collective-permute-start(bf16[256,1024]{1,0:T(8,128)(2,1)} %param.8), channel_id=1, source_target_pairs={{0,1},{1,2},{2,3},{3,4},{4,5},{5,6},{6,7},{7,8},{8,9},{9,10},{10,1... | collective-permute-start | bytes 1572872 | tf_op jit(solution)/shard_map/ppermute | solution.py:15
  6.7 0.7 broadcast_add_fusion
  7.4 1.9 %collective-permute-start.3 = (s32[256]{0:T(256)S(1)}, s32[256]{0:T(256)S(1)}, u32[]{:S(2)}, u32[]{:S(2)}) collective-permute-start(s32[256]{0:T(256)S(1)} %broadcast_add_fusion), channel_id=1, source_target_pairs={{0,3},{1,4},{2,5},{3,6},{4,7},{5,8},{6,9},{7,10},{8,11},{9,12},{10... | collective-permute-start | bytes 3080 | tf_op jit(solution)/shard_map/ppermute | solution.py:15
  9.3 1.9 %collective-permute-start.4 = (s32[256]{0:T(256)S(1)}, s32[256]{0:T(256)S(1)}, u32[]{:S(2)}, u32[]{:S(2)}) collective-permute-start(s32[256]{0:T(256)S(1)} %broadcast_add_fusion), channel_id=1, source_target_pairs={{0,2},{1,3},{2,4},{3,5},{4,6},{5,7},{6,8},{7,9},{8,10},{9,11},{10,... | collective-permute-start | bytes 3080 | tf_op jit(solution)/shard_map/ppermute | solution.py:15
  11.2 14.7 %collective-permute-done.3 = s32[256]{0:T(256)S(1)} collective-permute-done((s32[256]{0:T(256)S(1)}, s32[256]{0:T(256)S(1)}, u32[]{:S(2)}, u32[]{:S(2)}) %collective-permute-start.3) | collective-permute-done | bytes 1056 | tf_op jit(solution)/shard_map/ppermute | solution.py:15
  26.0 4.5 %collective-permute-start.5 = (s32[256]{0:T(256)S(1)}, s32[256]{0:T(256)S(1)}, u32[]{:S(2)}, u32[]{:S(2)}) collective-permute-start(s32[256]{0:T(256)S(1)} %broadcast_add_fusion), channel_id=1, source_target_pairs={{0,1},{1,2},{2,3},{3,4},{4,5},{5,6},{6,7},{7,8},{8,9},{9,10},{10,1... | collective-permute-start | bytes 3080 | tf_op jit(solution)/shard_map/ppermute | solution.py:15
  30.5 1.2 copy.10
  31.7 0.0 collective-permute-done.4
  31.7 1.9 %collective-permute-start.6 = (bf16[256,1024]{0,1:T(8,128)(2,1)S(1)}, bf16[256,1024]{0,1:T(8,128)(2,1)}, u32[]{:S(2)}, u32[]{:S(2)}) collective-permute-start(bf16[256,1024]{0,1:T(8,128)(2,1)S(1)} %copy.10), channel_id=1, source_target_pairs={{0,3},{1,4},{2,5},{3,6},{4,7},{5,8},{6,9},{7,10},{8,11},{9,12},{10... | collective-permute-start | bytes 1572872 | tf_op jit(solution)/shard_map/ppermute | solution.py:15
  33.7 3.0 %collective-permute-done.5 = s32[256]{0:T(256)S(1)} collective-permute-done((s32[256]{0:T(256)S(1)}, s32[256]{0:T(256)S(1)}, u32[]{:S(2)}, u32[]{:S(2)}) %collective-permute-start.5) | collective-permute-done | bytes 1056 | tf_op jit(solution)/shard_map/ppermute | solution.py:15
  36.6 4.8 %collective-permute-start.7 = (bf16[256,1024]{0,1:T(8,128)(2,1)S(1)}, bf16[256,1024]{0,1:T(8,128)(2,1)}, u32[]{:S(2)}, u32[]{:S(2)}) collective-permute-start(bf16[256,1024]{0,1:T(8,128)(2,1)S(1)} %copy.10), channel_id=1, source_target_pairs={{0,2},{1,3},{2,4},{3,5},{4,6},{5,7},{6,8},{7,9},{8,10},{9,11},{10,... | collective-permute-start | bytes 1572872 | tf_op jit(solution)/shard_map/ppermute | solution.py:15
  41.5 0.0 collective-permute-done
  41.5 0.0 copy-start.1
  41.5 1.9 %collective-permute-start.8 = (bf16[256,1024]{0,1:T(8,128)(2,1)S(1)}, bf16[256,1024]{0,1:T(8,128)(2,1)}, u32[]{:S(2)}, u32[]{:S(2)}) collective-permute-start(bf16[256,1024]{0,1:T(8,128)(2,1)S(1)} %copy.10), channel_id=1, source_target_pairs={{0,1},{1,2},{2,3},{3,4},{4,5},{5,6},{6,7},{7,8},{8,9},{9,10},{10,1... | collective-permute-start | bytes 1572872 | tf_op jit(solution)/shard_map/ppermute | solution.py:15
  43.4 0.0 copy-start
  43.5 6.4 %copy.14 = bf16[256,8192]{0,1:T(8,128)(2,1)} copy(bf16[256,8192]{1,0:T(8,128)(2,1)} %param.6) | data formatting | bytes 8388608 | tf_op args[0]
  49.9 0.0 copy-done.1
  49.9 0.0 collective-permute-done.1
  49.9 0.0 copy-start.2
  49.9 0.8 copy-done.2
  50.7 0.0 collective-permute-done.2
  50.7 0.0 copy-done
  50.7 1.5 pad_maximum_fusion
  52.3 2.6 %copy.9 = bf16[1024,1024]{0,1:T(8,128)(2,1)} copy(bf16[1024,1024]{1,0:T(8,128)(2,1)S(1)} %pad_maximum_fusion) | data formatting | bytes 4194304 | tf_op jit(solution)/shard_map/concatenate | solution.py:69
  54.9 0.0 collective-permute-done.6
  54.9 11.6 %collective-permute-done.7 = bf16[256,1024]{0,1:T(8,128)(2,1)} collective-permute-done((bf16[256,1024]{0,1:T(8,128)(2,1)S(1)}, bf16[256,1024]{0,1:T(8,128)(2,1)}, u32[]{:S(2)}, u32[]{:S(2)}) %collective-permute-start.7) | collective-permute-done | bytes 524320 | tf_op jit(solution)/shard_map/ppermute | solution.py:15
  66.5 3.9 %collective-permute-done.8 = bf16[256,1024]{0,1:T(8,128)(2,1)} collective-permute-done((bf16[256,1024]{0,1:T(8,128)(2,1)S(1)}, bf16[256,1024]{0,1:T(8,128)(2,1)}, u32[]{:S(2)}, u32[]{:S(2)}) %collective-permute-start.8) | collective-permute-done | bytes 524320 | tf_op jit(solution)/shard_map/ppermute | solution.py:15
  70.4 1.6 pad_maximum_fusion.1
  72.0 86.4 %while.11 = (s32[]{:T(128)}, bf16[8,256,8,128]{1,3,2,0:T(8,128)(2,1)}, bf16[8,1024,128]{1,2,0:T(8,128)(2,1)}, bf16[8,1024,128]{1,2,0:T(8,128)(2,1)S(1)}, bf16[8,...) while((s32[]{:T(128)}, ...), condition=%wide.region_3.4_spmd.clone, body=%wide.region_0.3_spmd.clone.sunk | while | flops 1626342400 | bytes 12084317 | solution.py:53
  72.0 0.3 fusion.103
  72.3 6.8 %fusion.104 = (f32[8,256]{1,0:T(8,128)S(1)}, bf16[8,256,1024]{1,2,0:T(8,128)(2,1)}) fusion(pred[256,1024]{0,1:T(8,128)(4,1)S(1)} %fusion.103, bf16[8,256,8,128]{1,3,2,0:T(8,128)(2,1)} %get-tuple-element.162, s32[]{:T(128)} %get-tuple-element.149, bf16[8,1024,128]{1,2,0:T(8,128)(2,1)S(1)} %get-tuple-element.161), kind=kOutput, calls=%fused_computation.65.clone.1 | convolution fusion | flops 1088422912 | bytes 6301696 | tf_op jit(solution)/shard_map/while/body/eval_jaxpr/sub | solution.py:47
  79.1 3.8 %fusion.105 = bf16[8,256,8,128]{1,3,2,0:T(8,128)(2,1)} fusion(bf16[8,256,8,128]{1,3,2,0:T(8,128)(2,1)} %get-tuple-element.150, s32[]{:T(128)} %get-tuple-element.149, bf16[8,256,1024]{1,2,0:T(8,128)(2,1)} %get-tuple-element.138, f32[256,8]{0,1:T(8,128)S(1)} %bitcast.109, bf16[8,1024,128]{1,2,0:T(8,128)(2,1)} %get-tuple-element.160), kind=kOutput, calls=%fused_computation.16.clone.1 | convolution fusion | flops 537133056 | bytes 5514240 | tf_op jit(solution)/shard_map/while/body/eval_jaxpr/qtl,ld->tqd/dot_general | solution.py:50
  82.9 0.2 fusion.103
  83.1 6.7 %fusion.104 = (f32[8,256]{1,0:T(8,128)S(1)}, bf16[8,256,1024]{1,2,0:T(8,128)(2,1)}) fusion(pred[256,1024]{0,1:T(8,128)(4,1)S(1)} %fusion.103, bf16[8,256,8,128]{1,3,2,0:T(8,128)(2,1)} %get-tuple-element.162, s32[]{:T(128)} %get-tuple-element.149, bf16[8,1024,128]{1,2,0:T(8,128)(2,1)S(1)} %get-tuple-element.161), kind=kOutput, calls=%fused_computation.65.clone.1 | convolution fusion | flops 1088422912 | bytes 6301696 | tf_op jit(solution)/shard_map/while/body/eval_jaxpr/sub | solution.py:47
  89.9 3.8 %fusion.105 = bf16[8,256,8,128]{1,3,2,0:T(8,128)(2,1)} fusion(bf16[8,256,8,128]{1,3,2,0:T(8,128)(2,1)} %get-tuple-element.150, s32[]{:T(128)} %get-tuple-element.149, bf16[8,256,1024]{1,2,0:T(8,128)(2,1)} %get-tuple-element.138, f32[256,8]{0,1:T(8,128)S(1)} %bitcast.109, bf16[8,1024,128]{1,2,0:T(8,128)(2,1)} %get-tuple-element.160), kind=kOutput, calls=%fused_computation.16.clone.1 | convolution fusion | flops 537133056 | bytes 5514240 | tf_op jit(solution)/shard_map/while/body/eval_jaxpr/qtl,ld->tqd/dot_general | solution.py:50
  93.7 0.2 fusion.103
  93.9 6.7 %fusion.104 = (f32[8,256]{1,0:T(8,128)S(1)}, bf16[8,256,1024]{1,2,0:T(8,128)(2,1)}) fusion(pred[256,1024]{0,1:T(8,128)(4,1)S(1)} %fusion.103, bf16[8,256,8,128]{1,3,2,0:T(8,128)(2,1)} %get-tuple-element.162, s32[]{:T(128)} %get-tuple-element.149, bf16[8,1024,128]{1,2,0:T(8,128)(2,1)S(1)} %get-tuple-element.161), kind=kOutput, calls=%fused_computation.65.clone.1 | convolution fusion | flops 1088422912 | bytes 6301696 | tf_op jit(solution)/shard_map/while/body/eval_jaxpr/sub | solution.py:47
  100.6 3.8 %fusion.105 = bf16[8,256,8,128]{1,3,2,0:T(8,128)(2,1)} fusion(bf16[8,256,8,128]{1,3,2,0:T(8,128)(2,1)} %get-tuple-element.150, s32[]{:T(128)} %get-tuple-element.149, bf16[8,256,1024]{1,2,0:T(8,128)(2,1)} %get-tuple-element.138, f32[256,8]{0,1:T(8,128)S(1)} %bitcast.109, bf16[8,1024,128]{1,2,0:T(8,128)(2,1)} %get-tuple-element.160), kind=kOutput, calls=%fused_computation.16.clone.1 | convolution fusion | flops 537133056 | bytes 5514240 | tf_op jit(solution)/shard_map/while/body/eval_jaxpr/qtl,ld->tqd/dot_general | solution.py:50
  104.4 0.2 fusion.103
  104.7 6.7 %fusion.104 = (f32[8,256]{1,0:T(8,128)S(1)}, bf16[8,256,1024]{1,2,0:T(8,128)(2,1)}) fusion(pred[256,1024]{0,1:T(8,128)(4,1)S(1)} %fusion.103, bf16[8,256,8,128]{1,3,2,0:T(8,128)(2,1)} %get-tuple-element.162, s32[]{:T(128)} %get-tuple-element.149, bf16[8,1024,128]{1,2,0:T(8,128)(2,1)S(1)} %get-tuple-element.161), kind=kOutput, calls=%fused_computation.65.clone.1 | convolution fusion | flops 1088422912 | bytes 6301696 | tf_op jit(solution)/shard_map/while/body/eval_jaxpr/sub | solution.py:47
  111.4 3.8 %fusion.105 = bf16[8,256,8,128]{1,3,2,0:T(8,128)(2,1)} fusion(bf16[8,256,8,128]{1,3,2,0:T(8,128)(2,1)} %get-tuple-element.150, s32[]{:T(128)} %get-tuple-element.149, bf16[8,256,1024]{1,2,0:T(8,128)(2,1)} %get-tuple-element.138, f32[256,8]{0,1:T(8,128)S(1)} %bitcast.109, bf16[8,1024,128]{1,2,0:T(8,128)(2,1)} %get-tuple-element.160), kind=kOutput, calls=%fused_computation.16.clone.1 | convolution fusion | flops 537133056 | bytes 5514240 | tf_op jit(solution)/shard_map/while/body/eval_jaxpr/qtl,ld->tqd/dot_general | solution.py:50
  115.2 0.2 fusion.103
  115.5 6.7 %fusion.104 = (f32[8,256]{1,0:T(8,128)S(1)}, bf16[8,256,1024]{1,2,0:T(8,128)(2,1)}) fusion(pred[256,1024]{0,1:T(8,128)(4,1)S(1)} %fusion.103, bf16[8,256,8,128]{1,3,2,0:T(8,128)(2,1)} %get-tuple-element.162, s32[]{:T(128)} %get-tuple-element.149, bf16[8,1024,128]{1,2,0:T(8,128)(2,1)S(1)} %get-tuple-element.161), kind=kOutput, calls=%fused_computation.65.clone.1 | convolution fusion | flops 1088422912 | bytes 6301696 | tf_op jit(solution)/shard_map/while/body/eval_jaxpr/sub | solution.py:47
  122.2 3.8 %fusion.105 = bf16[8,256,8,128]{1,3,2,0:T(8,128)(2,1)} fusion(bf16[8,256,8,128]{1,3,2,0:T(8,128)(2,1)} %get-tuple-element.150, s32[]{:T(128)} %get-tuple-element.149, bf16[8,256,1024]{1,2,0:T(8,128)(2,1)} %get-tuple-element.138, f32[256,8]{0,1:T(8,128)S(1)} %bitcast.109, bf16[8,1024,128]{1,2,0:T(8,128)(2,1)} %get-tuple-element.160), kind=kOutput, calls=%fused_computation.16.clone.1 | convolution fusion | flops 537133056 | bytes 5514240 | tf_op jit(solution)/shard_map/while/body/eval_jaxpr/qtl,ld->tqd/dot_general | solution.py:50
  126.0 0.2 fusion.103
  126.3 6.8 %fusion.104 = (f32[8,256]{1,0:T(8,128)S(1)}, bf16[8,256,1024]{1,2,0:T(8,128)(2,1)}) fusion(pred[256,1024]{0,1:T(8,128)(4,1)S(1)} %fusion.103, bf16[8,256,8,128]{1,3,2,0:T(8,128)(2,1)} %get-tuple-element.162, s32[]{:T(128)} %get-tuple-element.149, bf16[8,1024,128]{1,2,0:T(8,128)(2,1)S(1)} %get-tuple-element.161), kind=kOutput, calls=%fused_computation.65.clone.1 | convolution fusion | flops 1088422912 | bytes 6301696 | tf_op jit(solution)/shard_map/while/body/eval_jaxpr/sub | solution.py:47
  133.0 3.8 %fusion.105 = bf16[8,256,8,128]{1,3,2,0:T(8,128)(2,1)} fusion(bf16[8,256,8,128]{1,3,2,0:T(8,128)(2,1)} %get-tuple-element.150, s32[]{:T(128)} %get-tuple-element.149, bf16[8,256,1024]{1,2,0:T(8,128)(2,1)} %get-tuple-element.138, f32[256,8]{0,1:T(8,128)S(1)} %bitcast.109, bf16[8,1024,128]{1,2,0:T(8,128)(2,1)} %get-tuple-element.160), kind=kOutput, calls=%fused_computation.16.clone.1 | convolution fusion | flops 537133056 | bytes 5514240 | tf_op jit(solution)/shard_map/while/body/eval_jaxpr/qtl,ld->tqd/dot_general | solution.py:50
  136.8 0.2 fusion.103
  137.1 6.7 %fusion.104 = (f32[8,256]{1,0:T(8,128)S(1)}, bf16[8,256,1024]{1,2,0:T(8,128)(2,1)}) fusion(pred[256,1024]{0,1:T(8,128)(4,1)S(1)} %fusion.103, bf16[8,256,8,128]{1,3,2,0:T(8,128)(2,1)} %get-tuple-element.162, s32[]{:T(128)} %get-tuple-element.149, bf16[8,1024,128]{1,2,0:T(8,128)(2,1)S(1)} %get-tuple-element.161), kind=kOutput, calls=%fused_computation.65.clone.1 | convolution fusion | flops 1088422912 | bytes 6301696 | tf_op jit(solution)/shard_map/while/body/eval_jaxpr/sub | solution.py:47
  143.8 3.8 %fusion.105 = bf16[8,256,8,128]{1,3,2,0:T(8,128)(2,1)} fusion(bf16[8,256,8,128]{1,3,2,0:T(8,128)(2,1)} %get-tuple-element.150, s32[]{:T(128)} %get-tuple-element.149, bf16[8,256,1024]{1,2,0:T(8,128)(2,1)} %get-tuple-element.138, f32[256,8]{0,1:T(8,128)S(1)} %bitcast.109, bf16[8,1024,128]{1,2,0:T(8,128)(2,1)} %get-tuple-element.160), kind=kOutput, calls=%fused_computation.16.clone.1 | convolution fusion | flops 537133056 | bytes 5514240 | tf_op jit(solution)/shard_map/while/body/eval_jaxpr/qtl,ld->tqd/dot_general | solution.py:50
  147.6 0.2 fusion.103
  147.9 6.7 %fusion.104 = (f32[8,256]{1,0:T(8,128)S(1)}, bf16[8,256,1024]{1,2,0:T(8,128)(2,1)}) fusion(pred[256,1024]{0,1:T(8,128)(4,1)S(1)} %fusion.103, bf16[8,256,8,128]{1,3,2,0:T(8,128)(2,1)} %get-tuple-element.162, s32[]{:T(128)} %get-tuple-element.149, bf16[8,1024,128]{1,2,0:T(8,128)(2,1)S(1)} %get-tuple-element.161), kind=kOutput, calls=%fused_computation.65.clone.1 | convolution fusion | flops 1088422912 | bytes 6301696 | tf_op jit(solution)/shard_map/while/body/eval_jaxpr/sub | solution.py:47
  154.6 3.8 %fusion.105 = bf16[8,256,8,128]{1,3,2,0:T(8,128)(2,1)} fusion(bf16[8,256,8,128]{1,3,2,0:T(8,128)(2,1)} %get-tuple-element.150, s32[]{:T(128)} %get-tuple-element.149, bf16[8,256,1024]{1,2,0:T(8,128)(2,1)} %get-tuple-element.138, f32[256,8]{0,1:T(8,128)S(1)} %bitcast.109, bf16[8,1024,128]{1,2,0:T(8,128)(2,1)} %get-tuple-element.160), kind=kOutput, calls=%fused_computation.16.clone.1 | convolution fusion | flops 537133056 | bytes 5514240 | tf_op jit(solution)/shard_map/while/body/eval_jaxpr/qtl,ld->tqd/dot_general | solution.py:50
  158.4 6.6 %copy.17 = bf16[256,64,128]{2,1,0:T(8,128)(2,1)} copy(bf16[256,64,128]{0,2,1:T(8,128)(2,1)} %bitcast.106) | data formatting | bytes 8388608 | tf_op jit(solution)/shard_map/convert_element_type | solution.py:54
  165.0 3.4 %convolution_convert_fusion = bf16[256,128,64]{1,2,0:T(8,128)(2,1)S(1)} fusion(bf16[256,64,128]{2,1,0:T(8,128)(2,1)} %copy.17), kind=kOutput, calls=%fused_computation.37 | convolution fusion | flops 270643200 | bytes 8388608 | tf_op jit(solution)/shard_map/hk,tkd->thd/dot_general | solution.py:55
  168.4 10.2 %copy.23 = bf16[32,8,64,128]{3,1,2,0:T(8,128)(2,1)} copy(bf16[32,8,64,128]{3,2,1,0:T(8,128)(2,1)S(1)} %bitcast.104) | data formatting | bytes 8388608
  (3 shorter events, 0.0 us)
Async XLA Ops:
  0.0 41.5 %collective-permute-start = (bf16[256,1024]{1,0:T(8,128)(2,1)}, bf16[256,1024]{1,0:T(8,128)(2,1)S(1)}, u32[]{:S(2)}, u32[]{:S(2)}) collective-permute-start(bf16[256,1024]{1,0:T(8,128)(2,1)} %param.8), channel_id=1, source_target_pairs={{0,3},{1,4},{2,5},{3,6},{4,7},{5,8},{6,9},{7,10},{8,11},{9,12},{10... | collective-permute-start | bytes 1572872 | tf_op jit(solution)/shard_map/ppermute | solution.py:15
  2.8 47.1 %collective-permute-start.1 = (bf16[256,1024]{1,0:T(8,128)(2,1)}, bf16[256,1024]{1,0:T(8,128)(2,1)S(1)}, u32[]{:S(2)}, u32[]{:S(2)}) collective-permute-start(bf16[256,1024]{1,0:T(8,128)(2,1)} %param.8), channel_id=1, source_target_pairs={{0,2},{1,3},{2,4},{3,5},{4,6},{5,7},{6,8},{7,9},{8,10},{9,11},{10,... | collective-permute-start | bytes 1572872 | tf_op jit(solution)/shard_map/ppermute | solution.py:15
  4.8 45.9 %collective-permute-start.2 = (bf16[256,1024]{1,0:T(8,128)(2,1)}, bf16[256,1024]{1,0:T(8,128)(2,1)}, u32[]{:S(2)}, u32[]{:S(2)}) collective-permute-start(bf16[256,1024]{1,0:T(8,128)(2,1)} %param.8), channel_id=1, source_target_pairs={{0,1},{1,2},{2,3},{3,4},{4,5},{5,6},{6,7},{7,8},{8,9},{9,10},{10,1... | collective-permute-start | bytes 1572872 | tf_op jit(solution)/shard_map/ppermute | solution.py:15
  7.4 18.6 %collective-permute-start.3 = (s32[256]{0:T(256)S(1)}, s32[256]{0:T(256)S(1)}, u32[]{:S(2)}, u32[]{:S(2)}) collective-permute-start(s32[256]{0:T(256)S(1)} %broadcast_add_fusion), channel_id=1, source_target_pairs={{0,3},{1,4},{2,5},{3,6},{4,7},{5,8},{6,9},{7,10},{8,11},{9,12},{10... | collective-permute-start | bytes 3080 | tf_op jit(solution)/shard_map/ppermute | solution.py:15
  9.3 22.4 %collective-permute-start.4 = (s32[256]{0:T(256)S(1)}, s32[256]{0:T(256)S(1)}, u32[]{:S(2)}, u32[]{:S(2)}) collective-permute-start(s32[256]{0:T(256)S(1)} %broadcast_add_fusion), channel_id=1, source_target_pairs={{0,2},{1,3},{2,4},{3,5},{4,6},{5,7},{6,8},{7,9},{8,10},{9,11},{10,... | collective-permute-start | bytes 3080 | tf_op jit(solution)/shard_map/ppermute | solution.py:15
  26.0 10.7 %collective-permute-start.5 = (s32[256]{0:T(256)S(1)}, s32[256]{0:T(256)S(1)}, u32[]{:S(2)}, u32[]{:S(2)}) collective-permute-start(s32[256]{0:T(256)S(1)} %broadcast_add_fusion), channel_id=1, source_target_pairs={{0,1},{1,2},{2,3},{3,4},{4,5},{5,6},{6,7},{7,8},{8,9},{9,10},{10,1... | collective-permute-start | bytes 3080 | tf_op jit(solution)/shard_map/ppermute | solution.py:15
  31.7 23.2 %collective-permute-start.6 = (bf16[256,1024]{0,1:T(8,128)(2,1)S(1)}, bf16[256,1024]{0,1:T(8,128)(2,1)}, u32[]{:S(2)}, u32[]{:S(2)}) collective-permute-start(bf16[256,1024]{0,1:T(8,128)(2,1)S(1)} %copy.10), channel_id=1, source_target_pairs={{0,3},{1,4},{2,5},{3,6},{4,7},{5,8},{6,9},{7,10},{8,11},{9,12},{10... | collective-permute-start | bytes 1572872 | tf_op jit(solution)/shard_map/ppermute | solution.py:15
  36.6 29.9 %collective-permute-start.7 = (bf16[256,1024]{0,1:T(8,128)(2,1)S(1)}, bf16[256,1024]{0,1:T(8,128)(2,1)}, u32[]{:S(2)}, u32[]{:S(2)}) collective-permute-start(bf16[256,1024]{0,1:T(8,128)(2,1)S(1)} %copy.10), channel_id=1, source_target_pairs={{0,2},{1,3},{2,4},{3,5},{4,6},{5,7},{6,8},{7,9},{8,10},{9,11},{10,... | collective-permute-start | bytes 1572872 | tf_op jit(solution)/shard_map/ppermute | solution.py:15
  41.5 8.4 %copy-start.1 = (bf16[256,1024]{1,0:T(8,128)(2,1)}, bf16[256,1024]{1,0:T(8,128)(2,1)S(1)}, u32[]{:S(2)}) copy-start(bf16[256,1024]{1,0:T(8,128)(2,1)S(1)} %collective-permute-done) | copy-start | bytes 1572868
  41.5 28.9 %collective-permute-start.8 = (bf16[256,1024]{0,1:T(8,128)(2,1)S(1)}, bf16[256,1024]{0,1:T(8,128)(2,1)}, u32[]{:S(2)}, u32[]{:S(2)}) collective-permute-start(bf16[256,1024]{0,1:T(8,128)(2,1)S(1)} %copy.10), channel_id=1, source_target_pairs={{0,1},{1,2},{2,3},{3,4},{4,5},{5,6},{6,7},{7,8},{8,9},{9,10},{10,1... | collective-permute-start | bytes 1572872 | tf_op jit(solution)/shard_map/ppermute | solution.py:15
  43.4 7.3 %copy-start = (bf16[256,1024]{1,0:T(8,128)(2,1)S(1)}, bf16[256,1024]{1,0:T(8,128)(2,1)}, u32[]{:S(2)}) copy-start(bf16[256,1024]{1,0:T(8,128)(2,1)} %param.8) | copy-start | bytes 1572868
  49.9 0.8 copy-start.2
where the time goes:
time: 180 us; the launch traced here: 179 us
  matrix products  87.7 us (49%)
  waiting for transfers between devices  33.2 us (18%)
  local copies, waits for them, and re-layouts  27.8 us (15%)
  starting transfers between devices  23.7 us (13%)
  other arithmetic  5.87 us (3%)
    sub x8, matrix products, one_head(): weights = jnp.where(allowed[None], jnp.exp(scores - top), 0.0)  53.9 us
    ppermute x9, waiting for transfers between devices, passed_along(): return lax.ppermute(array, axis, pairs)  33.2 us
    dot_general x8, matrix products, one_head(): jnp.einsum('qtl,ld->tqd', probs, vh, preferred_element_type=jnp.float32)  30.4 us
    ppermute x9, starting transfers between devices, passed_along(): return lax.ppermute(array, axis, pairs)  23.7 us
    unnamed x9, local copies, waits for them, and re-layouts  18.7 us
    convert_element_type x1, local copies, waits for them, and re-layouts, attend(): jnp.transpose(outs, (1, 0, 2, 3)).reshape(count, HEADS, HD)  6.55 us
  transfers between devices with their start and end apart: 9, of which 4 were waited for; matrix products, arithmetic and copies ran while one was open for 7% of the time, Pallas kernels for 0%

commit v1 on v0

v1 whole, which is shorter than its diff:
```python
import functools
import math

import jax
import jax.numpy as jnp
from jax import lax
from jax.experimental import pallas as pl
from jax.experimental.pallas import tpu as pltpu
from jax.sharding import PartitionSpec as P

HEADS = 64
KVH = 8
HD = 128
PRIOR = 3
GROUP = HEADS // KVH
AXIS = "context"
LOW = -1e30
SCALE = math.log2(math.e) / math.sqrt(HD)


def butterfly(parts):
    parts = list(parts)
    step = 1
    while step < len(parts):
        for a in range(len(parts)):
            if a & step == 0:
                low, high = parts[a], parts[a + step]
                parts[a], parts[a + step] = low + high, low - high
        step *= 2
    return parts


def attend_kernel(n, tok, q_hbm, k_hbm, v_hbm, seg_hbm, acc, qv, kv, segw, bias, q_sem, kv_sem, seg_sem, send_sem, recv_sem, seg_send, seg_recv):
    me = lax.axis_index(AXIS)
    pos = lax.rem(me, 4)
    odd = lax.rem(me, 2)
    partner = me + 1 - 2 * odd
    own = pl.ds(PRIOR * tok, tok)

    def slot(d):
        return pl.ds((PRIOR - d) * tok, tok)

    def local_kv(h):
        cols = pl.ds(h * HD, HD)
        return (
            pltpu.make_async_copy(k_hbm.at[:, cols], kv.at[h, 0, own, :], kv_sem.at[0, h]),
            pltpu.make_async_copy(v_hbm.at[:, cols], kv.at[h, 1, own, :], kv_sem.at[1, h]),
        )

    def local_q(g):
        cols = pl.ds(g * GROUP * HD, GROUP * HD)
        return pltpu.make_async_copy(q_hbm.at[:, cols], qv.at[:, cols], q_sem.at[g])

    local_seg = pltpu.make_async_copy(seg_hbm, segw.at[PRIOR], seg_sem)
    local_seg.start()
    for h in range(KVH):
        for copy in local_kv(h):
            copy.start()
    for g in range(KVH):
        local_q(g).start()

    barrier = pltpu.get_barrier_semaphore()
    for d in range(1, PRIOR + 1):
        for near in (me - d, me + d):
            @pl.when((near >= 0) & (near < n))
            def _():
                pl.semaphore_signal(barrier, inc=1, device_id={AXIS: near}, device_id_type=pl.DeviceIdType.MESH)

    for d in range(1, PRIOR + 1):
        @pl.when(me < d)
        def _():
            kv[:, :, slot(d), :] = jnp.zeros((KVH, 2, tok, HD), jnp.bfloat16)
            segw[PRIOR - d] = jnp.full((1, tok), -1, jnp.int32)

    pl.semaphore_wait(barrier, jnp.minimum(me, PRIOR) + jnp.minimum(n - 1 - me, PRIOR))

    def push(h, source, target, flow, to):
        return pltpu.make_async_remote_copy(
            src_ref=kv.at[h, :, source, :],
            dst_ref=kv.at[h, :, slot(target), :],
            send_sem=send_sem.at[flow],
            recv_sem=recv_sem.at[target - 1, h],
            device_id={AXIS: to},
            device_id_type=pl.DeviceIdType.MESH,
        )

    def seg_push(d):
        return pltpu.make_async_remote_copy(
            src_ref=segw.at[PRIOR],
            dst_ref=segw.at[PRIOR - d],
            send_sem=seg_send.at[d - 1],
            recv_sem=seg_recv.at[d - 1],
            device_id={AXIS: me + d},
            device_id_type=pl.DeviceIdType.MESH,
        )

    own_far = ((pos != 3) & (me + 2 < n), (odd == 1) & (me + 3 < n), odd == 0)

    def send_own(h):
        for d, flow, when in ((2, 0, own_far[0]), (3, 1, own_far[1]), (1, 2, own_far[2])):
            @pl.when(when)
            def _():
                push(h, own, d, flow, me + d).start()

    def wait_arrival(h, d):
        push(h, own, d, 0, partner).wait_recv()

    has = tuple(me >= d for d in range(1, PRIOR + 1))
    relays = (pos == 2) & has[2]

    def stage_a(h):
        @pl.when(relays)
        def _():
            wait_arrival(h, 3)
            push(h, slot(3), 2, 1, me - 1).start()

    def stage_b(h):
        @pl.when(has[1])
        def _():
            wait_arrival(h, 2)

            @pl.when(odd == 0)
            def _():
                push(h, slot(2), 3, 3, partner).start()

            @pl.when(odd == 1)
            def _():
                push(h, slot(2), 1, 3, partner).start()

    def stage_c(h):
        @pl.when(has[0])
        def _():
            wait_arrival(h, 1)

        @pl.when(has[2] & (pos != 2))
        def _():
            wait_arrival(h, 3)

    local_seg.wait()
    for d in range(1, PRIOR + 1):
        @pl.when(me + d < n)
        def _():
            seg_push(d).start()

    def start_own(h, carry):
        for copy in local_kv(h):
            copy.wait()
        send_own(h)
        return carry

    lax.fori_loop(0, KVH, start_own, 0)

    for d in range(1, PRIOR + 1):
        @pl.when(me >= d)
        def _():
            seg_push(d).wait_recv()

    seg_q = jnp.transpose(jnp.broadcast_to(segw[PRIOR], (128, tok)))
    for block in range((PRIOR + 1) * tok // 128):
        shard, part = divmod(block * 128, tok)
        seg_k = jnp.broadcast_to(segw[shard][:, part:part + 128], (tok, 128))
        key_idx = lax.broadcasted_iota(jnp.int32, (tok, 128), 1) + block * 128
        query_idx = lax.broadcasted_iota(jnp.int32, (tok, 128), 0) + PRIOR * tok
        allowed = (seg_k == seg_q) & (key_idx <= query_idx)
        bias[:, block * 128:(block + 1) * 128] = jnp.where(allowed, 0.0, LOW)

    half = tok // 2
    span = PRIOR * tok + half

    def one_group(g):
        ones = jnp.ones((span, HD), jnp.bfloat16)
        done = []
        for j in range(GROUP):
            pieces = []
            for rb in range(2):
                rows = pl.ds(rb * half, half)
                keys = pl.ds(rb * half, span)
                q = qv[rows, pl.ds(pl.multiple_of((g * GROUP + j) * HD, HD), HD)]
                s = lax.dot_general(q, kv[g, 0, keys, :], (((1,), (1,)), ((), ())), preferred_element_type=jnp.float32)
                s = s + bias[rows, keys]
                top = jnp.max(s, axis=-1, keepdims=True)
                p = jnp.exp2((s - top) * SCALE).astype(jnp.bfloat16)
                wide = jnp.concatenate([kv[g, 1, keys, :], ones], axis=1)
                o = jnp.dot(p, wide, preferred_element_type=jnp.float32)
                pieces.append((o[:, :HD] / o[:, HD:]).astype(jnp.bfloat16).astype(jnp.float32))
            done.append(pieces)
        for rb in range(2):
            mixed = butterfly([done[j][rb] for j in range(GROUP)])
            for j in range(GROUP):
                acc[g, j, pl.ds(rb * half, half), :] = mixed[j]

    stage_a(0)
    stage_a(1)
    stage_b(0)

    def step(g, carry):
        @pl.when(g + 2 < KVH)
        def _():
            stage_a(g + 2)

        @pl.when(g + 1 < KVH)
        def _():
            stage_b(g + 1)

        stage_c(g)
        local_q(g).wait()
        one_group(g)
        return carry

    lax.fori_loop(0, KVH, step, 0)

    def drain(flow):
        pltpu.make_async_remote_copy(
            src_ref=kv.at[:, :, own, :],
            dst_ref=kv.at[:, :, own, :],
            send_sem=send_sem.at[flow],
            recv_sem=recv_sem.at[0, 0],
            device_id={AXIS: partner},
            device_id_type=pl.DeviceIdType.MESH,
        ).wait_send()

    for flow, when in enumerate((own_far[0], own_far[1] | relays, own_far[2], has[1])):
        @pl.when(when)
        def _():
            drain(flow)

    for d in range(1, PRIOR + 1):
        @pl.when(me + d < n)
        def _():
            seg_push(d).wait_send()


def mix_kernel(rows, acc, out):
    start = pl.multiple_of(pl.program_id(0) * rows, rows)
    for j in range(GROUP):
        mixed = butterfly([acc[g, j, pl.ds(start, rows), :] for g in range(KVH)])
        for g in range(KVH):
            col = (g * GROUP + j) * HD
            out[:, col:col + HD] = (mixed[g] * (1.0 / math.sqrt(HEADS))).astype(jnp.bfloat16)


def per_device(n, queries, keys, values, segments):
    tok = queries.shape[0]
    hbm = pl.BlockSpec(memory_space=pl.ANY)
    vmem = pl.BlockSpec(memory_space=pltpu.VMEM)
    acc = pl.pallas_call(
        functools.partial(attend_kernel, n, tok),
        out_shape=pltpu.VMEM((KVH, GROUP, tok, HD), jnp.float32),
        in_specs=[hbm] * 4,
        out_specs=vmem,
        scratch_shapes=[
            pltpu.VMEM((tok, HEADS * HD), jnp.bfloat16),
            pltpu.VMEM((KVH, 2, (PRIOR + 1) * tok, HD), jnp.bfloat16),
            pltpu.VMEM((PRIOR + 1, 1, tok), jnp.int32),
            pltpu.VMEM((tok, (PRIOR + 1) * tok), jnp.float32),
            pltpu.SemaphoreType.DMA((KVH,)),
            pltpu.SemaphoreType.DMA((2, KVH)),
            pltpu.SemaphoreType.DMA,
            pltpu.SemaphoreType.DMA((4,)),
            pltpu.SemaphoreType.DMA((PRIOR, KVH)),
            pltpu.SemaphoreType.DMA((PRIOR,)),
            pltpu.SemaphoreType.DMA((PRIOR,)),
        ],
        compiler_params=pltpu.CompilerParams(
            collective_id=0, has_side_effects=True, vmem_limit_bytes=50 * 2**20
        ),
        name="attend",
    )(queries, keys, values, segments.reshape(1, tok))
    rows = 32
    return pl.pallas_call(
        functools.partial(mix_kernel, rows),
        grid=(tok // rows,),
        out_shape=jax.ShapeDtypeStruct((tok, HEADS * HD), jnp.bfloat16),
        in_specs=[vmem],
        out_specs=pl.BlockSpec((rows, HEADS * HD), lambda i: (i, 0)),
        compiler_params=pltpu.CompilerParams(vmem_limit_bytes=16 * 2**20),
        name="mix",
    )(acc)


def solution(mesh):
    spec = P(("groups", AXIS), None)
    return jax.shard_map(
        functools.partial(per_device, mesh.shape[AXIS]),
        mesh=mesh,
        in_specs=(spec, spec, spec, P(("groups", AXIS))),
        out_specs=spec,
        check_vma=False,
    )
```

time: 180 us -> 44.6 us (0.25)
  the two profiles are of different devices: /device:TPU:24 before, /device:TPU:25 now
where the time goes in v1:
time: 44.6 us; the launch traced here: 44.5 us
  Pallas kernels  44.5 us (100%)
    pallas_call x1, Pallas kernels, per_device(): pl.pallas_call(functools.partial(attend_kernel, n, tok), out_shape=pltpu....  40.3 us
    pallas_call x1, Pallas kernels, per_device(): pl.pallas_call(functools.partial(mix_kernel, rows), grid=(tok // rows,),...  4.21 us

profile of v1, /device:TPU:25, one launch (start us, length us, event | category | flops | bytes accessed | tf_op | source)
XLA Modules:
  0.0 44.5 jit_solution(5254863954588104894)
XLA Ops:
  0.0 40.3 %attend.1.acc = f32[8,8,256,128]{3,2,1,0:T(8,128)S(1)} custom-call(bf16[256,8192]{1,0:T(8,128)(2,1)} %q_hbm.1, bf16[256,1024]{1,0:T(8,128)(2,1)} %k_hbm.1, bf16[256,1024]{1,0:T(8,128)(2,1)} %v_hbm.1, s32[1,256]{1,0:T(1,128)} %bitcast.1), custom_call_target="tpu_custom_call" | custom-call | tf_op jit(solution)/shard_map/attend/pallas_call | solution.py:246
  40.3 4.2 %mix.1 = bf16[256,8192]{1,0:T(8,128)(2,1)} custom-call(f32[8,8,256,128]{3,2,1,0:T(8,128)S(1)} %attend.1.acc), custom_call_target="tpu_custom_call" | custom-call | tf_op jit(solution)/shard_map/mix/pallas_call | solution.py:270

commit v2 on v1

--- a/solution.py
+++ b/solution.py
@@ -15,6 +15,9 @@
 GROUP = HEADS // KVH
 AXIS = "context"
 LOW = -1e30
+BATCH = 8
+CHUNKS = 2 * KVH
+AHEAD = 3
 SCALE = math.log2(math.e) / math.sqrt(HD)
 
 
@@ -43,8 +46,8 @@
     def local_kv(h):
         cols = pl.ds(h * HD, HD)
         return (
-            pltpu.make_async_copy(k_hbm.at[:, cols], kv.at[h, 0, own, :], kv_sem.at[0, h]),
-            pltpu.make_async_copy(v_hbm.at[:, cols], kv.at[h, 1, own, :], kv_sem.at[1, h]),
+            pltpu.make_async_copy(k_hbm.at[:, cols], kv.at[2 * h, own, :], kv_sem.at[2 * h]),
+            pltpu.make_async_copy(v_hbm.at[:, cols], kv.at[2 * h + 1, own, :], kv_sem.at[2 * h + 1]),
         )
 
     def local_q(g):
@@ -69,15 +72,15 @@
     for d in range(1, PRIOR + 1):
         @pl.when(me < d)
         def _():
-            kv[:, :, slot(d), :] = jnp.zeros((KVH, 2, tok, HD), jnp.bfloat16)
+            kv[:, slot(d), :] = jnp.zeros((CHUNKS, tok, HD), jnp.bfloat16)
             segw[PRIOR - d] = jnp.full((1, tok), -1, jnp.int32)
 
     pl.semaphore_wait(barrier, jnp.minimum(me, PRIOR) + jnp.minimum(n - 1 - me, PRIOR))
 
     def push(h, source, target, flow, to):
         return pltpu.make_async_remote_copy(
-            src_ref=kv.at[h, :, source, :],
-            dst_ref=kv.at[h, :, slot(target), :],
+            src_ref=kv.at[h, source, :],
+            dst_ref=kv.at[h, slot(target), :],
             send_sem=send_sem.at[flow],
             recv_sem=recv_sem.at[target - 1, h],
             device_id={AXIS: to},
@@ -96,11 +99,20 @@
 
     own_far = ((pos != 3) & (me + 2 < n), (odd == 1) & (me + 3 < n), odd == 0)
 
+    paced = (pos == 2) & (me + 2 < n)
+
     def send_own(h):
-        for d, flow, when in ((2, 0, own_far[0]), (3, 1, own_far[1]), (1, 2, own_far[2])):
-            @pl.when(when)
-            def _():
-                push(h, own, d, flow, me + d).start()
+        @pl.when(own_far[0] & ((pos != 2) | (h < AHEAD)))
+        def _():
+            push(h, own, 2, 0, me + 2).start()
+
+        @pl.when(own_far[1])
+        def _():
+            push(h, own, 3, 1, me + 3).start()
+
+        @pl.when(own_far[2])
+        def _():
+            push(h, own, 1, 2, me + 1).start()
 
     def wait_arrival(h, d):
         push(h, own, d, 0, partner).wait_recv()
@@ -113,6 +125,10 @@
         def _():
             wait_arrival(h, 3)
             push(h, slot(3), 2, 1, me - 1).start()
+
+        @pl.when(paced & (h + AHEAD < CHUNKS))
+        def _():
+            push(h + AHEAD, own, 2, 0, me + 2).start()
 
     def stage_b(h):
         @pl.when(has[1])
@@ -143,9 +159,11 @@
             seg_push(d).start()
 
     def start_own(h, carry):
-        for copy in local_kv(h):
-            copy.wait()
-        send_own(h)
+        key_copy, value_copy = local_kv(h)
+        key_copy.wait()
+        send_own(2 * h)
+        value_copy.wait()
+        send_own(2 * h + 1)
         return carry
 
     lax.fori_loop(0, KVH, start_own, 0)
@@ -167,52 +185,61 @@
     half = tok // 2
     span = PRIOR * tok + half
 
-    def one_group(g):
+    def score(g, rb, j0):
+        rows, keys = pl.ds(rb * half, half), pl.ds(rb * half, span)
+        q = jnp.concatenate([qv[rows, pl.ds(pl.multiple_of((g * GROUP + j) * HD, HD), HD)] for j in range(j0, j0 + BATCH)], axis=0)
+        return lax.dot_general(q, kv[2 * g, keys, :], (((1,), (1,)), ((), ())), preferred_element_type=jnp.float32)
+
+    def soften(s, rb):
+        s = s.reshape(BATCH, half, span) + bias[pl.ds(rb * half, half), pl.ds(rb * half, span)][None]
+        top = jnp.max(s, axis=-1, keepdims=True)
+        return jnp.exp2((s - top) * SCALE).astype(jnp.bfloat16).reshape(BATCH * half, span)
+
+    def gather(g, p, rb):
         ones = jnp.ones((span, HD), jnp.bfloat16)
-        done = []
-        for j in range(GROUP):
-            pieces = []
-            for rb in range(2):
-                rows = pl.ds(rb * half, half)
-                keys = pl.ds(rb * half, span)
-                q = qv[rows, pl.ds(pl.multiple_of((g * GROUP + j) * HD, HD), HD)]
-                s = lax.dot_general(q, kv[g, 0, keys, :], (((1,), (1,)), ((), ())), preferred_element_type=jnp.float32)
-                s = s + bias[rows, keys]
-                top = jnp.max(s, axis=-1, keepdims=True)
-                p = jnp.exp2((s - top) * SCALE).astype(jnp.bfloat16)
-                wide = jnp.concatenate([kv[g, 1, keys, :], ones], axis=1)
-                o = jnp.dot(p, wide, preferred_element_type=jnp.float32)
-                pieces.append((o[:, :HD] / o[:, HD:]).astype(jnp.bfloat16).astype(jnp.float32))
-            done.append(pieces)
+        wide = jnp.concatenate([kv[2 * g + 1, pl.ds(rb * half, span), :], ones], axis=1)
+        o = jnp.dot(p, wide, preferred_element_type=jnp.float32)
+        o = (o[:, :HD] / o[:, HD:]).astype(jnp.bfloat16).astype(jnp.float32) * (1.0 / math.sqrt(HEADS))
+        return [o[j * half:(j + 1) * half] for j in range(BATCH)]
+
+    def attend_group(g):
         for rb in range(2):
-            mixed = butterfly([done[j][rb] for j in range(GROUP)])
+            mixed = butterfly(gather(g, soften(score(g, rb, 0), rb), rb))
             for j in range(GROUP):
                 acc[g, j, pl.ds(rb * half, half), :] = mixed[j]
 
-    stage_a(0)
-    stage_a(1)
-    stage_b(0)
+    early = pos != 1
+
+    def relay(c):
+        @pl.when(early & (c < CHUNKS))
+        def _():
+            stage_a(c)
+            stage_b(c)
+
+    relay(0)
+    relay(1)
 
     def step(g, carry):
-        @pl.when(g + 2 < KVH)
-        def _():
-            stage_a(g + 2)
-
-        @pl.when(g + 1 < KVH)
-        def _():
-            stage_b(g + 1)
-
-        stage_c(g)
+        relay(2 * g + 2)
+        relay(2 * g + 3)
+
+        @pl.when(pos == 1)
+        def _():
+            stage_b(2 * g)
+            stage_b(2 * g + 1)
+
+        stage_c(2 * g)
+        stage_c(2 * g + 1)
         local_q(g).wait()
-        one_group(g)
+        attend_group(g)
         return carry
 
     lax.fori_loop(0, KVH, step, 0)
 
     def drain(flow):
         pltpu.make_async_remote_copy(
-            src_ref=kv.at[:, :, own, :],
-            dst_ref=kv.at[:, :, own, :],
+            src_ref=kv.at[:, own, :],
+            dst_ref=kv.at[:, own, :],
             send_sem=send_sem.at[flow],
             recv_sem=recv_sem.at[0, 0],
             device_id={AXIS: partner},
@@ -230,13 +257,29 @@
             seg_push(d).wait_send()
 
 
-def mix_kernel(rows, acc, out):
-    start = pl.multiple_of(pl.program_id(0) * rows, rows)
-    for j in range(GROUP):
-        mixed = butterfly([acc[g, j, pl.ds(start, rows), :] for g in range(KVH)])
-        for g in range(KVH):
-            col = (g * GROUP + j) * HD
-            out[:, col:col + HD] = (mixed[g] * (1.0 / math.sqrt(HEADS))).astype(jnp.bfloat16)
+def mix_kernel(rows, acc, out, held, sem):
+    count = out.shape[0] // rows
+
+    def leave(i):
+        part = pl.ds(pl.multiple_of(i * rows, rows), rows)
+        return pltpu.make_async_copy(held.at[part], out.at[part], sem.at[i])
+
+    def body(i, carry):
+        part = pl.ds(pl.multiple_of(i * rows, rows), rows)
+        for j in range(GROUP):
+            mixed = butterfly([acc[g, j, part, :] for g in range(KVH)])
+            for g in range(KVH):
+                col = (g * GROUP + j) * HD
+                held[part, col:col + HD] = mixed[g].astype(jnp.bfloat16)
+        leave(i).start()
+        return carry
+
+    def finish(i, carry):
+        leave(i).wait()
+        return carry
+
+    lax.fori_loop(0, count, body, 0)
+    lax.fori_loop(0, count, finish, 0)
 
 
 def per_device(n, queries, keys, values, segments):
@@ -250,14 +293,14 @@
         out_specs=vmem,
         scratch_shapes=[
             pltpu.VMEM((tok, HEADS * HD), jnp.bfloat16),
-            pltpu.VMEM((KVH, 2, (PRIOR + 1) * tok, HD), jnp.bfloat16),
+            pltpu.VMEM((CHUNKS, (PRIOR + 1) * tok, HD), jnp.bfloat16),
             pltpu.VMEM((PRIOR + 1, 1, tok), jnp.int32),
             pltpu.VMEM((tok, (PRIOR + 1) * tok), jnp.float32),
             pltpu.SemaphoreType.DMA((KVH,)),
-            pltpu.SemaphoreType.DMA((2, KVH)),
+            pltpu.SemaphoreType.DMA((CHUNKS,)),
             pltpu.SemaphoreType.DMA,
             pltpu.SemaphoreType.DMA((4,)),
-            pltpu.SemaphoreType.DMA((PRIOR, KVH)),
+            pltpu.SemaphoreType.DMA((PRIOR, CHUNKS)),
             pltpu.SemaphoreType.DMA((PRIOR,)),
             pltpu.SemaphoreType.DMA((PRIOR,)),
         ],
@@ -266,13 +309,16 @@
         ),
         name="attend",
     )(queries, keys, values, segments.reshape(1, tok))
-    rows = 32
+    rows = 16
     return pl.pallas_call(
         functools.partial(mix_kernel, rows),
-        grid=(tok // rows,),
         out_shape=jax.ShapeDtypeStruct((tok, HEADS * HD), jnp.bfloat16),
         in_specs=[vmem],
-        out_specs=pl.BlockSpec((rows, HEADS * HD), lambda i: (i, 0)),
+        out_specs=hbm,
+        scratch_shapes=[
+            pltpu.VMEM((tok, HEADS * HD), jnp.bfloat16),
+            pltpu.SemaphoreType.DMA((tok // rows,)),
+        ],
         compiler_params=pltpu.CompilerParams(vmem_limit_bytes=16 * 2**20),
         name="mix",
     )(acc)

time: 44.6 us -> 41.4 us (0.928)
  the two profiles are of different devices: /device:TPU:25 before, /device:TPU:24 now
where the time goes in v2:
time: 41.4 us; the launch traced here: 41.2 us
  Pallas kernels  41.2 us (100%)
    pallas_call x1, Pallas kernels, per_device(): pl.pallas_call(functools.partial(attend_kernel, n, tok), out_shape=pltpu....  38.8 us
    pallas_call x1, Pallas kernels, per_device(): pl.pallas_call(functools.partial(mix_kernel, rows), out_shape=jax.ShapeDt...  2.39 us

profile of v2, /device:TPU:24, one launch (start us, length us, event | category | flops | bytes accessed | tf_op | source)
XLA Modules:
  0.0 41.2 jit_solution(2990799295813755301)
XLA Ops:
  0.0 38.8 %attend.1.acc = f32[8,8,256,128]{3,2,1,0:T(8,128)S(1)} custom-call(bf16[256,8192]{1,0:T(8,128)(2,1)} %q_hbm.1, bf16[256,1024]{1,0:T(8,128)(2,1)} %k_hbm.1, bf16[256,1024]{1,0:T(8,128)(2,1)} %v_hbm.1, s32[1,256]{1,0:T(1,128)} %bitcast.1), custom_call_target="tpu_custom_call" | custom-call | tf_op jit(solution)/shard_map/attend/pallas_call | solution.py:289
  38.8 2.4 %mix.1 = bf16[256,8192]{1,0:T(8,128)(2,1)} custom-call(f32[8,8,256,128]{3,2,1,0:T(8,128)S(1)} %attend.1.acc), custom_call_target="tpu_custom_call" | custom-call | tf_op jit(solution)/shard_map/mix/pallas_call | solution.py:313
